TPU v7x, 32 devices: a whole 2x2x4 slice. The times are simulated.
32 devices in a mesh: fsdp: 4 (over z), replica: 2 (over x), ctx: 4 (over y, core).
Axes of the slice: x: 2, y: 2, z: 4, core: 2. Of those that a mesh axis runs over, the one named last changes fastest.
Arguments:
- hidden_in: bfloat16 [8, 1088, 2048], P(('fsdp', 'replica'), 'ctx'), may hold values from -6 to 6
- memory_rows: bfloat16 [8, 50, 2048], P(('fsdp', 'replica')), may hold values from -6 to 6
- seg_len: int32 [8], P(('fsdp', 'replica')), may hold values from 519 to 1038, as said below
- out_grad: bfloat16 [8, 1088, 2048], P(('fsdp', 'replica'), 'ctx'), may hold values from -6 to 6
- first_gain: bfloat16 [2048], P('fsdp'), may hold values from 0.5 to 1.5
- first_shift: bfloat16 [2048], P('fsdp'), may hold values from -1 to 1
- qkv_weight: bfloat16 [2048, 6144], P('fsdp'), may hold values from -0.125 to 0.125
- query_bias: bfloat16 [2048], P('fsdp'), may hold values from -4 to 4
- value_bias: bfloat16 [2048], P('fsdp'), may hold values from -2.5 to 2.5
- out_weight: bfloat16 [2048, 2048], P('fsdp'), may hold values from -2 to 2
- out_bias: bfloat16 [2048], P('fsdp'), may hold values from -1 to 1
- second_gain: bfloat16 [2048], P('fsdp'), may hold values from 0.5 to 1.5
- second_shift: bfloat16 [2048], P('fsdp'), may hold values from -1 to 1
- up_weight: bfloat16 [2048, 8192], P('fsdp'), may hold values from -0.125 to 0.125
- up_bias: bfloat16 [8192], P('fsdp'), may hold values from -1 to 1
- down_weight: bfloat16 [8192, 2048], P('fsdp'), may hold values from -0.0625 to 0.0625
- down_bias: bfloat16 [2048], P('fsdp'), may hold values from -1 to 1
Outputs:
- output: bfloat16 [8, 1088, 2048], P(('fsdp', 'replica'), 'ctx')
- input_grad: float32 [8, 1088, 2048], P(('fsdp', 'replica'), 'ctx')
- memory_grad: float32 [8, 50, 2048], P(('fsdp', 'replica'))
- first_gain_grad: float32 [2048], P('fsdp')
- first_shift_grad: float32 [2048], P('fsdp')
- qkv_weight_grad: float32 [2048, 6144], P('fsdp')
- query_bias_grad: float32 [2048], P('fsdp')
- value_bias_grad: float32 [2048], P('fsdp')
- out_weight_grad: float32 [2048, 2048], P('fsdp')
- out_bias_grad: float32 [2048], P('fsdp')
- second_gain_grad: float32 [2048], P('fsdp')
- second_shift_grad: float32 [2048], P('fsdp')
- up_weight_grad: float32 [2048, 8192], P('fsdp')
- up_bias_grad: float32 [8192], P('fsdp')
- down_weight_grad: float32 [8192, 2048], P('fsdp')
- down_bias_grad: float32 [2048], P('fsdp')
Inputs may be any that keep to these rules, and one draw needn't show every extreme that they name: Positions seg_len to 1037 of a segment are padding that no query uses as a key.
All inputs are finite; a program needn't handle non-finite values.
Results may differ from a plain program's by a relative error of at most 0.015.
Values may be sent and summed in bfloat16 or wider, within the bound.
No kernel may reach another device: no remote copies, remote signals or barrier semaphores. Data moves between devices by JAX's collectives and lax.ppermute only.
A program may use at most 512 MiB of HBM per device.

v0:
```python
import jax
import jax.numpy as jnp
from jax import lax
from jax.sharding import PartitionSpec as P

D = 2048
HEADS = 32
HEAD_DIM = 64
SUMM = 50
SEQ_LEN = 1088
SEG = 1038
epsilon = 1e-05
masked = -1e30


def smooth_unit(values):
    return jax.nn.gelu(values, approximate=False)


def layer_norm(inputs, weight, offset):
    average = jnp.mean(inputs, axis=-1, keepdims=True)
    centred = inputs - average
    spread = jnp.mean(centred * centred, axis=-1, keepdims=True)
    inverse = lax.rsqrt(spread + epsilon)
    normal = centred * inverse
    return (normal * weight + offset, normal, inverse)


def norm_back(upstream, normal, inverse, weight):
    scaled = upstream * weight
    centre_term = jnp.mean(scaled, axis=-1, keepdims=True)
    slope_term = jnp.mean(scaled * normal, axis=-1, keepdims=True)
    return (
        inverse * (scaled - centre_term - normal * slope_term),
        jnp.sum(upstream * normal, axis=0),
        jnp.sum(upstream, axis=0),
    )


def across(left, right):
    return lax.dot_general(
        left, right, (((0,), (0,)), ((), ())), preferred_element_type=jnp.float32
    )


def against(left, right):
    return lax.dot_general(
        left, right, (((1,), (1,)), ((), ())), preferred_element_type=jnp.float32
    )


def head_slice(array, block_index, block_width, head_group):
    piece = lax.dynamic_slice_in_dim(array, block_index * block_width, block_width, 2)
    return piece.reshape(piece.shape[0], piece.shape[1], head_group, block_width // head_group)


def shards(
    hidden_in,
    memory_rows,
    seg_len,
    out_grad,
    first_gain,
    first_shift,
    qkv_weight,
    query_bias,
    value_bias,
    out_weight,
    out_bias,
    second_gain,
    second_shift,
    up_weight,
    up_bias,
    down_weight,
    down_bias,
):
    gathered = (
        lax.all_gather(first_gain, "fsdp", axis=0, tiled=True),
        lax.all_gather(first_shift, "fsdp", axis=0, tiled=True),
        lax.all_gather(qkv_weight, "fsdp", axis=0, tiled=True),
        lax.all_gather(query_bias, "fsdp", axis=0, tiled=True),
        lax.all_gather(value_bias, "fsdp", axis=0, tiled=True),
        lax.all_gather(out_weight, "fsdp", axis=0, tiled=True),
        lax.all_gather(out_bias, "fsdp", axis=0, tiled=True),
        lax.all_gather(second_gain, "fsdp", axis=0, tiled=True),
        lax.all_gather(second_shift, "fsdp", axis=0, tiled=True),
        lax.all_gather(up_weight, "fsdp", axis=0, tiled=True),
        lax.all_gather(up_bias, "fsdp", axis=0, tiled=True),
        lax.all_gather(down_weight, "fsdp", axis=0, tiled=True),
        lax.all_gather(down_bias, "fsdp", axis=0, tiled=True),
    )
    gain_one = gathered[0].astype(jnp.float32)
    shift_one = gathered[1].astype(jnp.float32)
    bias_query = gathered[3].astype(jnp.float32)
    bias_value = gathered[4].astype(jnp.float32)
    bias_out = gathered[6].astype(jnp.float32)
    gain_two = gathered[7].astype(jnp.float32)
    shift_two = gathered[8].astype(jnp.float32)
    bias_up = gathered[10].astype(jnp.float32)
    bias_down = gathered[12].astype(jnp.float32)
    weight_qkv = gathered[2]
    weight_out = gathered[5]
    weight_up = gathered[9]
    weight_down = gathered[11]
    groups = hidden_in.shape[0]
    span_rows = hidden_in.shape[1]
    row_count = groups * span_rows
    mem_count = groups * SUMM
    key_count = SUMM + SEQ_LEN
    head_group = min(8, HEADS)
    group_count = HEADS // head_group
    block_width = head_group * HEAD_DIM
    tokens = hidden_in.reshape(row_count, D).astype(jnp.float32)
    normed, normal_one, inverse_one = layer_norm(tokens, gain_one, shift_one)
    normed_low = normed.astype(jnp.bfloat16)
    memory = memory_rows.reshape(mem_count, D).astype(jnp.float32)
    mem_normed, mem_normal, mem_inverse = layer_norm(memory, gain_one, shift_one)
    mem_low = mem_normed.astype(jnp.bfloat16)
    projected = jnp.dot(normed_low, weight_qkv, preferred_element_type=jnp.float32)
    mem_projected = jnp.dot(mem_low, weight_qkv[:, D:], preferred_element_type=jnp.float32)
    query = (
        ((projected[:, :D] + bias_query) * 0.125).astype(jnp.bfloat16).reshape(groups, span_rows, D)
    )
    keys_local = projected[:, D : 2 * D].astype(jnp.bfloat16).reshape(groups, span_rows, D)
    values_local = (
        (projected[:, 2 * D :] + bias_value).astype(jnp.bfloat16).reshape(groups, span_rows, D)
    )
    mem_keys = mem_projected[:, :D].astype(jnp.bfloat16).reshape(groups, SUMM, D)
    mem_values = (mem_projected[:, D:] + bias_value).astype(jnp.bfloat16).reshape(groups, SUMM, D)
    keys_seq, values_seq = (
        lax.all_gather(keys_local, "ctx", axis=1, tiled=True),
        lax.all_gather(values_local, "ctx", axis=1, tiled=True),
    )
    keys_all = jnp.concatenate([mem_keys, keys_seq], axis=1)
    values_all = jnp.concatenate([mem_values, values_seq], axis=1)
    positions = lax.axis_index("ctx") * span_rows + jnp.arange(span_rows, dtype=jnp.int32)
    key_places = jnp.arange(SEQ_LEN, dtype=jnp.int32)
    causal = key_places[None, :] <= positions[:, None]
    present = (key_places[None, :] < seg_len[:, None]) | (key_places[None, :] >= SEG)
    allowed = jnp.concatenate(
        [jnp.ones((groups, span_rows, SUMM), dtype=bool), causal[None] & present[:, None, :]],
        axis=2,
    )[:, None]

    def attend(block_index):
        query_block = head_slice(query, block_index, block_width, head_group)
        key_block = head_slice(keys_all, block_index, block_width, head_group)
        value_block = head_slice(values_all, block_index, block_width, head_group)
        scores = jnp.einsum(
            "gqhd,gkhd->ghqk", query_block, key_block, preferred_element_type=jnp.float32
        )
        scores = jnp.where(allowed, scores, masked)
        largest = jnp.max(scores, axis=-1, keepdims=True)
        expanded = jnp.exp(scores - largest)
        totals = jnp.sum(expanded, axis=-1, keepdims=True)
        weights_low = (expanded / totals).astype(jnp.bfloat16)
        mixed_rows = jnp.einsum(
            "ghqk,gkhd->gqhd", weights_low, value_block, preferred_element_type=jnp.float32
        )
        return (mixed_rows.reshape(groups, span_rows, block_width), largest + jnp.log(totals))

    mixed_blocks, log_totals = lax.map(attend, jnp.arange(group_count))
    attended = jnp.moveaxis(mixed_blocks, 0, 2).reshape(row_count, D).astype(jnp.bfloat16)
    branch = jnp.dot(attended, weight_out, preferred_element_type=jnp.float32) + bias_out
    middle = tokens + branch
    normed_two, normal_two, inverse_two = layer_norm(middle, gain_two, shift_two)
    normed_two_low = normed_two.astype(jnp.bfloat16)
    upper = jnp.dot(normed_two_low, weight_up, preferred_element_type=jnp.float32) + bias_up
    active_float, smooth_pull = jax.vjp(smooth_unit, upper)
    active = active_float.astype(jnp.bfloat16)
    output = (
        (middle + (jnp.dot(active, weight_down, preferred_element_type=jnp.float32) + bias_down))
        .astype(jnp.bfloat16)
        .reshape(groups, span_rows, D)
    )
    again = (
        lax.all_gather(qkv_weight, "fsdp", axis=0, tiled=True),
        lax.all_gather(out_weight, "fsdp", axis=0, tiled=True),
        lax.all_gather(up_weight, "fsdp", axis=0, tiled=True),
        lax.all_gather(down_weight, "fsdp", axis=0, tiled=True),
    )
    back_qkv = again[0]
    back_out = again[1]
    back_up = again[2]
    back_down = again[3]
    cotangent = out_grad.reshape(row_count, D)
    cot_float = cotangent.astype(jnp.float32)
    down_part = lax.psum_scatter(
        across(active, cotangent).astype(jnp.bfloat16), "fsdp", scatter_dimension=0, tiled=True
    ).astype(jnp.float32)
    hidden_grad = against(cotangent, back_down)
    upper_grad = smooth_pull(hidden_grad)[0].astype(jnp.bfloat16)
    up_part = lax.psum_scatter(
        across(normed_two_low, upper_grad).astype(jnp.bfloat16),
        "fsdp",
        scatter_dimension=0,
        tiled=True,
    ).astype(jnp.float32)
    normed_two_grad = against(upper_grad, back_up)
    middle_norm_grad, gain_two_grad, shift_two_grad = norm_back(
        normed_two_grad, normal_two, inverse_two, gain_two
    )
    middle_grad = cot_float + middle_norm_grad
    branch_grad = middle_grad.astype(jnp.bfloat16)
    out_weight_grad = across(attended, branch_grad)
    mixed_grad = against(branch_grad, back_out).astype(jnp.bfloat16).reshape(groups, span_rows, D)

    def attend_back(block_index):
        query_block = head_slice(query, block_index, block_width, head_group)
        key_block = head_slice(keys_all, block_index, block_width, head_group)
        value_block = head_slice(values_all, block_index, block_width, head_group)
        grad_block = head_slice(mixed_grad, block_index, block_width, head_group)
        scores = jnp.einsum(
            "gqhd,gkhd->ghqk", query_block, key_block, preferred_element_type=jnp.float32
        )
        scores = jnp.where(allowed, scores, masked)
        weights = jnp.exp(scores - log_totals[block_index])
        value_grad = jnp.einsum(
            "ghqk,gqhd->gkhd",
            weights.astype(jnp.bfloat16),
            grad_block,
            preferred_element_type=jnp.float32,
        )
        weight_grad = jnp.einsum(
            "gqhd,gkhd->ghqk", grad_block, value_block, preferred_element_type=jnp.float32
        )
        centre = jnp.sum(weights * weight_grad, axis=-1, keepdims=True)
        score_grad = (weights * (weight_grad - centre)).astype(jnp.bfloat16)
        query_grad = jnp.einsum(
            "ghqk,gkhd->gqhd", score_grad, key_block, preferred_element_type=jnp.float32
        )
        key_grad = jnp.einsum(
            "ghqk,gqhd->gkhd", score_grad, query_block, preferred_element_type=jnp.float32
        )
        return (
            query_grad.reshape(groups, span_rows, block_width),
            key_grad.reshape(groups, key_count, block_width),
            value_grad.reshape(groups, key_count, block_width),
        )

    query_blocks, key_blocks, value_blocks = lax.map(attend_back, jnp.arange(group_count))
    query_grad_all = jnp.moveaxis(query_blocks, 0, 2).reshape(groups, span_rows, D)
    key_grad_all = jnp.moveaxis(key_blocks, 0, 2).reshape(groups, key_count, D)
    value_grad_all = jnp.moveaxis(value_blocks, 0, 2).reshape(groups, key_count, D)
    key_sums, value_sums = (
        lax.psum_scatter(key_grad_all[:, SUMM:], "ctx", scatter_dimension=1, tiled=True),
        lax.psum_scatter(value_grad_all[:, SUMM:], "ctx", scatter_dimension=1, tiled=True),
    )
    mem_key_sums, mem_value_sums = lax.psum(
        (key_grad_all[:, :SUMM], value_grad_all[:, :SUMM]), "ctx"
    )
    qkv_grad = jnp.concatenate(
        [
            query_grad_all.astype(jnp.bfloat16) * 0.125,
            key_sums.astype(jnp.bfloat16),
            value_sums.astype(jnp.bfloat16),
        ],
        axis=2,
    ).reshape(row_count, 3 * D)
    mem_kv_grad = jnp.concatenate(
        [mem_key_sums.astype(jnp.bfloat16), mem_value_sums.astype(jnp.bfloat16)], axis=2
    ).reshape(mem_count, 2 * D)
    owner_flag = lax.axis_index("ctx") == 0
    first_owner = owner_flag.astype(jnp.float32)
    owned_mem_grad = jnp.where(owner_flag, mem_kv_grad, jnp.zeros_like(mem_kv_grad))
    mem_rows_grad = jnp.concatenate(
        [jnp.zeros((mem_count, D), jnp.bfloat16), owned_mem_grad], axis=1
    )
    qkv_weight_grad = across(
        jnp.concatenate([normed_low, mem_low], axis=0),
        jnp.concatenate([qkv_grad, mem_rows_grad], axis=0),
    )
    query_bias_grad = jnp.sum(qkv_grad[:, :D].astype(jnp.float32), axis=0)
    value_bias_grad = jnp.sum(qkv_grad[:, 2 * D :].astype(jnp.float32), axis=0) + jnp.sum(
        owned_mem_grad[:, D:].astype(jnp.float32), axis=0
    )
    out_bias_grad = jnp.sum(branch_grad.astype(jnp.float32), axis=0)
    up_bias_grad = jnp.sum(upper_grad.astype(jnp.float32), axis=0)
    down_bias_grad = jnp.sum(cot_float, axis=0)
    normed_grad = against(qkv_grad, back_qkv)
    token_norm_grad, gain_one_tok, shift_one_tok = norm_back(
        normed_grad, normal_one, inverse_one, gain_one
    )
    mem_normed_grad = against(mem_kv_grad, back_qkv[:, D:])
    memory_norm_grad, gain_one_mem, shift_one_mem = norm_back(
        mem_normed_grad, mem_normal, mem_inverse, gain_one
    )
    gain_one_grad = gain_one_tok + first_owner * gain_one_mem
    shift_one_grad = shift_one_tok + first_owner * shift_one_mem
    input_grad = (middle_grad + token_norm_grad).reshape(groups, span_rows, D)
    memory_grad = memory_norm_grad.reshape(groups, SUMM, D)
    shares = (
        lax.psum_scatter(
            gain_one_grad.astype(jnp.bfloat16), "fsdp", scatter_dimension=0, tiled=True
        ).astype(jnp.float32),
        lax.psum_scatter(
            shift_one_grad.astype(jnp.bfloat16), "fsdp", scatter_dimension=0, tiled=True
        ).astype(jnp.float32),
        lax.psum_scatter(
            qkv_weight_grad.astype(jnp.bfloat16), "fsdp", scatter_dimension=0, tiled=True
        ).astype(jnp.float32),
        lax.psum_scatter(
            query_bias_grad.astype(jnp.bfloat16), "fsdp", scatter_dimension=0, tiled=True
        ).astype(jnp.float32),
        lax.psum_scatter(
            value_bias_grad.astype(jnp.bfloat16), "fsdp", scatter_dimension=0, tiled=True
        ).astype(jnp.float32),
        lax.psum_scatter(
            out_weight_grad.astype(jnp.bfloat16), "fsdp", scatter_dimension=0, tiled=True
        ).astype(jnp.float32),
        lax.psum_scatter(
            out_bias_grad.astype(jnp.bfloat16), "fsdp", scatter_dimension=0, tiled=True
        ).astype(jnp.float32),
        lax.psum_scatter(
            gain_two_grad.astype(jnp.bfloat16), "fsdp", scatter_dimension=0, tiled=True
        ).astype(jnp.float32),
        lax.psum_scatter(
            shift_two_grad.astype(jnp.bfloat16), "fsdp", scatter_dimension=0, tiled=True
        ).astype(jnp.float32),
        lax.psum_scatter(
            up_bias_grad.astype(jnp.bfloat16), "fsdp", scatter_dimension=0, tiled=True
        ).astype(jnp.float32),
        lax.psum_scatter(
            down_bias_grad.astype(jnp.bfloat16), "fsdp", scatter_dimension=0, tiled=True
        ).astype(jnp.float32),
    )
    summed = lax.psum(
        (
            shares[0],
            shares[1],
            shares[2],
            shares[3],
            shares[4],
            shares[5],
            shares[6],
            shares[7],
            shares[8],
            shares[9],
            shares[10],
            up_part,
            down_part,
        ),
        ("replica", "ctx"),
    )
    return (
        output,
        input_grad,
        memory_grad,
        summed[0],
        summed[1],
        summed[2],
        summed[3],
        summed[4],
        summed[5],
        summed[6],
        summed[7],
        summed[8],
        summed[11],
        summed[9],
        summed[12],
        summed[10],
    )


def solution(mesh):
    return jax.shard_map(
        shards,
        mesh=mesh,
        in_specs=(
            P(("fsdp", "replica"), "ctx", None),
            P(("fsdp", "replica"), None, None),
            P(("fsdp", "replica")),
            P(("fsdp", "replica"), "ctx", None),
            P("fsdp"),
            P("fsdp"),
            P("fsdp", None),
            P("fsdp"),
            P("fsdp"),
            P("fsdp", None),
            P("fsdp"),
            P("fsdp"),
            P("fsdp"),
            P("fsdp", None),
            P("fsdp"),
            P("fsdp", None),
            P("fsdp"),
        ),
        out_specs=(
            P(("fsdp", "replica"), "ctx", None),
            P(("fsdp", "replica"), "ctx", None),
            P(("fsdp", "replica"), None, None),
            P("fsdp"),
            P("fsdp"),
            P("fsdp", None),
            P("fsdp"),
            P("fsdp"),
            P("fsdp", None),
            P("fsdp"),
            P("fsdp"),
            P("fsdp"),
            P("fsdp", None),
            P("fsdp"),
            P("fsdp", None),
            P("fsdp"),
        ),
        check_vma=False,
    )
```

profile of v0, /device:TPU:1, one launch (start us, length us, event | category | flops | bytes accessed | tf_op | source)
XLA Modules:
  0.0 7154.1 jit_solution(2888771679025506342)
XLA Ops:
  8.7 10.3 all-gather.3
  29.7 36.0 all-gather.5
  66.3 33.2 all-gather.4
  100.8 336.6 %all-gather.17.cloned.1.call-done = bf16[2048,6144]{1,0:T(8,128)(2,1)} async-done(((bf16[512,6144]{1,0:T(8,128)(2,1)}), bf16[2048,6144]{1,0:T(8,128)(2,1)}) %all-gather.17.cloned.1.call-update) | async-done | bytes 25165840 | tf_op jit(solution)/shard_map/all_gather | solution.py:79
  437.4 11.9 fusion.87
  469.3 10.2 all_gather.61
  540.9 48.0 while.26
  589.0 88.8 %all-gather.19.cloned.1.call-done = bf16[2048,2048]{1,0:T(8,128)(2,1)} async-done(((bf16[512,2048]{1,0:T(8,128)(2,1)}), bf16[2048,2048]{1,0:T(8,128)(2,1)}) %all-gather.19.cloned.1.call-update) | async-done | bytes 8388624 | tf_op jit(solution)/shard_map/all_gather | solution.py:82
  686.1 552.7 %all-gather.21.cloned.1.call-done = bf16[2048,8192]{1,0:T(8,128)(2,1)} async-done(((bf16[512,8192]{1,0:T(8,128)(2,1)}), bf16[2048,8192]{1,0:T(8,128)(2,1)}) %all-gather.21.cloned.1.call-update) | async-done | bytes 33554448 | tf_op jit(solution)/shard_map/all_gather | solution.py:86
  1238.8 34.7 multiply_convert_fusion.1
  1273.5 526.4 %all-gather.23.cloned.1.call-done = bf16[8192,2048]{1,0:T(8,128)(2,1)} async-done(((bf16[2048,2048]{1,0:T(8,128)(2,1)}), bf16[8192,2048]{1,0:T(8,128)(2,1)}) %all-gather.23.cloned.1.call-update) | async-done | bytes 33554448 | tf_op jit(solution)/shard_map/all_gather | solution.py:88
  1799.8 36.5 fusion.83
  1836.4 17.0 multiply_reduce_fusion.1
  1870.2 188.6 %while.27 = (s32[]{:T(128)}, bf16[4,1,272,512]{2,3,1,0:T(8,128)(2,1)}, f32[4,1,1138,512]{2,3,1,0:T(8,128)}, f32[4,1,1138,512]{2,3,1,0:T(8,128)}, s32[4]{0:T(128)...) while((s32[]{:T(128)}, ...), condition=%wide.region_14.15_spmd, body=%wide.region_12.14_spmd.sunk | while | flops 1604632448 | bytes 115616344 | solution.py:240
  1893.0 10.1 multiply_convert_fusion.3
  1940.1 10.1 multiply_convert_fusion.3
  1987.2 10.1 multiply_convert_fusion.3
  2077.8 21.4 copy.74
  2099.3 21.4 copy.73
  2120.7 2492.1 %all-reduce.20 = (bf16[1,50,2048]{2,0,1:T(2,128)(2,1)S(1)}, bf16[1,50,2048]{2,0,1:T(2,128)(2,1)S(1)}, bf16[1,1088,2048]{2,0,1:T(2,128)(2,1)}, bf16[1,1088,2048]{2,0,1:T(2,128)(2,1)}) all-reduce(f32[1,50,2048]{2,0,1:T(1,128)S(1)} %copy.76, f32[1,50,2048]{2,0,1:T(1,128)S(1)} %copy.75, ...), channel_id=1, replica_groups=mesh['fsdp'=4,'replica'=2,'ctx'=4] {'ctx'}, use_global_device_ids=true, to_apply=%region_20.21 | all-reduce | flops 4661248 | bytes 27967488 | tf_op jit(solution)/shard_map/psum | solution.py:248
  4629.4 17.2 convolution_convert_fusion.2
  4648.3 24.3 convolution_convert_fusion.1
  4673.8 24.3 convolution_convert_fusion
  4698.8 11.8 all-gather.9
  4712.8 12.2 fusion.69
  4731.5 14.9 fusion.40
  4746.5 19.0 all-reduce.17
  4770.6 17.5 fusion.31
  4788.1 272.3 %reduce-scatter.9.cloned.1.call-done = bf16[512,6144]{1,0:T(8,128)(2,1)} async-done(((bf16[2048,6144]{1,0:T(8,128)(2,1)}), bf16[512,6144]{1,0:T(8,128)(2,1)}) %reduce-scatter.9.cloned.1.call-update) | async-done | bytes 6291472 | tf_op jit(solution)/shard_map/reduce_scatter | solution.py:298
  5060.4 556.3 %reduce-scatter.13.cloned.1.call-done = bf16[512,8192]{1,0:T(8,128)(2,1)} async-done(((bf16[2048,8192]{1,0:T(8,128)(2,1)}), bf16[512,8192]{1,0:T(8,128)(2,1)}) %reduce-scatter.13.cloned.1.call-update) | async-done | bytes 8388624
  5616.7 555.0 %reduce-scatter.15.cloned.1.call-done = bf16[2048,2048]{1,0:T(8,128)(2,1)} async-done(((bf16[8192,2048]{1,0:T(8,128)(2,1)}), bf16[2048,2048]{1,0:T(8,128)(2,1)}) %reduce-scatter.15.cloned.1.call-update) | async-done | bytes 8388624
  6171.8 975.3 %all-reduce.21 = (f32[512]{0:T(512)}, f32[512]{0:T(512)}, f32[512,6144]{1,0:T(8,128)}, f32[512]{0:T(512)}, f32[512]{0:T(512)}, /*index=5*/f32[512,2048]{1,0:T(8,...) all-reduce(f32[512]{0:T(512)S(1)} %dynamic-slice_convert_fusion.8, ...), channel_id=1, replica_groups=mesh['fsdp'=4,'replica'=2,'ctx'=4] {'replica','ctx'}, use_global_device_ids=true, to_apply=%region_26.27 | all-reduce | flops 12589056 | bytes 75546624 | tf_op jit(solution)/shard_map/psum | solution.py:326
  (348 shorter events, 362.5 us)
Async XLA Ops:
  7.2 92.4 %copy-start.2 = (bf16[1,272,2048]{2,1,0:T(8,128)(2,1)S(1)}, bf16[1,272,2048]{2,1,0:T(8,128)(2,1)}, u32[]{:S(2)}) copy-start(bf16[1,272,2048]{2,1,0:T(8,128)(2,1)} %param.21) | copy-start | bytes 3342340
  7.2 430.2 %all-gather.17.cloned.1.call-start = ((), (), s32[]{:S(2)}) async-start(), calls=%async_computation.4 | async-start | bytes 31457280 | tf_op jit(solution)/shard_map/all_gather | solution.py:79
  7.9 502.7 %all-gather.25.cloned.1.call-start = ((), (), s32[]{:S(2)}) async-start(), calls=%async_computation.10 | async-start | bytes 5570560 | tf_op jit(solution)/shard_map/all_gather | solution.py:131
  29.0 472.0 %copy-start.25 = (f32[4,1,512]{2,1,0:T(1,128)}, f32[4,1,512]{2,1,0:T(1,128)S(1)}, u32[]{:S(2)}) copy-start(f32[4,1,512]{2,1,0:T(1,128)S(1)} %convert_element_type.263) | copy-start | bytes 24580
  99.8 349.5 %copy-start.29 = (f32[272]{0:T(512)}, f32[272]{0:T(512)S(1)}, u32[]{:S(2)}) copy-start(f32[272]{0:T(512)S(1)} %broadcast_multiply_fusion.5) | copy-start | bytes 3268
  100.3 349.1 %copy-start.33 = (f32[272]{0:T(512)}, f32[272]{0:T(512)S(1)}, u32[]{:S(2)}) copy-start(f32[272]{0:T(512)S(1)} %add_rsqrt_fusion.1) | copy-start | bytes 3268
  100.8 348.6 %copy-start.18 = (bf16[272,2048]{1,0:T(8,128)(2,1)}, bf16[272,2048]{1,0:T(8,128)(2,1)S(1)}, u32[]{:S(2)}) copy-start(bf16[272,2048]{1,0:T(8,128)(2,1)S(1)} %fusion.34) | copy-start | bytes 3342340
  454.2 72.7 %all-gather.27.cloned.1.call-start = ((), (), s32[]{:S(2)}) async-start(), calls=%async_computation.11 | async-start | bytes 5570560 | tf_op jit(solution)/shard_map/all_gather | solution.py:130
  457.0 220.7 %all-gather.19.cloned.1.call-start = ((), (), s32[]{:S(2)}) async-start(), calls=%async_computation.5 | async-start | bytes 10485760 | tf_op jit(solution)/shard_map/all_gather | solution.py:82
  457.6 21.9 copy-start.49
  457.6 31.6 copy-start.50
  457.6 41.0 copy-start.53
  457.7 42.2 copy-start.17
  457.7 781.1 %all-gather.21.cloned.1.call-start = ((), (), s32[]{:S(2)}) async-start(), calls=%async_computation.6 | async-start | bytes 41943040 | tf_op jit(solution)/shard_map/all_gather | solution.py:86
  458.3 1341.6 %all-gather.23.cloned.1.call-start = ((), (), s32[]{:S(2)}) async-start(), calls=%async_computation.7 | async-start | bytes 41943040 | tf_op jit(solution)/shard_map/all_gather | solution.py:88
  458.8 4329.3 %reduce-scatter.11.cloned.1.call-start = ((), (), s32[]{:S(2)}) async-start(), calls=%async_computation.9 | async-start | bytes 10485760 | tf_op jit(solution)/shard_map/reduce_scatter | solution.py:307
  489.3 749.5 %copy-start.39 = (f32[4,1,512]{2,1,0:T(1,128)}, f32[4,1,512]{2,1,0:T(1,128)S(1)}, u32[]{:S(2)}) copy-start(f32[4,1,512]{2,1,0:T(1,128)S(1)} %convert_element_type.269) | copy-start | bytes 24580
  498.6 1354.8 %copy-start.27 = (f32[4,1,512]{2,1,0:T(1,128)}, f32[4,1,512]{2,1,0:T(1,128)S(1)}, u32[]{:S(2)}) copy-start(f32[4,1,512]{2,1,0:T(1,128)S(1)} %convert_element_type.268) | copy-start | bytes 24580
  589.0 95.4 %copy-start = (pred[1,1,272,1138]{3,2,1,0:T(8,128)(4,1)}, pred[1,1,272,1138]{3,2,1,0:T(8,128)(4,1)S(1)}, u32[]{:S(2)}) copy-start(pred[1,1,272,1138]{3,2,1,0:T(8,128)(4,1)S(1)} %get-tuple-element.553) | copy-start | bytes 928612
  589.0 95.4 %copy-start.7 = (bf16[1,272,2048]{1,2,0:T(8,128)(2,1)}, bf16[1,272,2048]{1,2,0:T(8,128)(2,1)S(1)}, u32[]{:S(2)}) copy-start(bf16[1,272,2048]{1,2,0:T(8,128)(2,1)S(1)} %get-tuple-element.562) | copy-start | bytes 3342340
  684.4 1169.1 %copy-start.31 = (f32[272]{0:T(512)}, f32[272]{0:T(512)S(1)}, u32[]{:S(2)}) copy-start(f32[272]{0:T(512)S(1)} %broadcast_multiply_fusion.4) | copy-start | bytes 3268
  686.1 1167.3 %copy-start.37 = (f32[272]{0:T(512)}, f32[272]{0:T(512)S(1)}, u32[]{:S(2)}) copy-start(f32[272]{0:T(512)S(1)} %add_rsqrt_fusion) | copy-start | bytes 3268
  1238.8 561.0 %copy-start.13 = (bf16[1,272,2048]{2,1,0:T(8,128)(2,1)S(1)}, bf16[1,272,2048]{2,1,0:T(8,128)(2,1)}, u32[]{:S(2)}) copy-start(bf16[1,272,2048]{2,1,0:T(8,128)(2,1)} %param.24) | copy-start | bytes 3342340
  1799.8 36.5 copy-start.5
  1836.4 17.1 copy-start.14
  1861.8 3198.6 %reduce-scatter.9.cloned.1.call-start = ((), (), s32[]{:S(2)}) async-start(), calls=%async_computation.8 | async-start | bytes 31457280 | tf_op jit(solution)/shard_map/reduce_scatter | solution.py:298
  4646.7 970.0 %reduce-scatter.13.cloned.1.call-start = ((), (), s32[]{:S(2)}) async-start(), calls=%async_computation.12 | async-start | bytes 41943040
  4672.6 1499.1 %reduce-scatter.15.cloned.1.call-start = ((), (), s32[]{:S(2)}) async-start(), calls=%async_computation.13 | async-start | bytes 41943040
  4712.8 18.7 copy-start.3
  4712.8 18.7 copy-start.30
  4712.8 18.7 copy-start.34
  4731.5 15.0 copy-start.35
  (43 other events, 279.8 us)
Sparse Core Ops, SparseCore 0:
  9.6 427.7 all-gather.16
  454.3 34.3 all-gather.24
  490.8 35.9 all-gather.26
  528.2 149.4 all-gather.18
  679.1 559.6 all-gather.20
  1240.2 559.5 all-gather.22
  1861.9 142.2 reduce-scatter.10
  4646.8 413.5 reduce-scatter.8
  5062.9 553.7 reduce-scatter.12
  5619.0 552.7 reduce-scatter.14
where the time goes:
time: 7170 us; the launch traced here: 7150 us
  blocking collectives  3630 us (51%)
  waiting for transfers between devices  2890 us (40%)
  matrix products  356 us (5%)
  local copies, waits for them, and re-layouts  161 us (2%)
  other arithmetic  84.4 us (1%)
    psum x1, blocking collectives, shards(): lax.psum((key_grad_all[:, :SUMM], value_grad_all[:, :SUMM]), 'ctx')  2490 us
    unnamed x12, waiting for transfers between devices  1110 us
    psum x1, blocking collectives, shards(): lax.psum((shares[0], shares[1], shares[2], shares[3], shares[4], shares[5...  975 us
    all_gather x1, waiting for transfers between devices, shards(): lax.all_gather(up_weight, 'fsdp', axis=0, tiled=True)  553 us
    all_gather x1, waiting for transfers between devices, shards(): lax.all_gather(down_weight, 'fsdp', axis=0, tiled=True)  526 us
    all_gather x1, waiting for transfers between devices, shards(): lax.all_gather(qkv_weight, 'fsdp', axis=0, tiled=True)  337 us
    reduce_scatter x1, waiting for transfers between devices, shards(): lax.psum_scatter(qkv_weight_grad.astype(jnp.bfloat16), 'fsdp', scatter_di...  272 us
  transfers between devices with their start and end apart: 10, of which 8 were waited for; matrix products, arithmetic and copies ran while one was open for 7% of the time, Pallas kernels for 0%

commit v1 on v0

--- a/solution.py
+++ b/solution.py
@@ -324,22 +324,25 @@
         ).astype(jnp.float32),
     )
     summed = lax.psum(
-        (
-            shares[0],
-            shares[1],
-            shares[2],
-            shares[3],
-            shares[4],
-            shares[5],
-            shares[6],
-            shares[7],
-            shares[8],
-            shares[9],
-            shares[10],
-            up_part,
-            down_part,
+        lax.psum(
+            (
+                shares[0],
+                shares[1],
+                shares[2],
+                shares[3],
+                shares[4],
+                shares[5],
+                shares[6],
+                shares[7],
+                shares[8],
+                shares[9],
+                shares[10],
+                up_part,
+                down_part,
+            ),
+            "ctx",
         ),
-        ("replica", "ctx"),
+        "replica",
     )
     return (
         output,

time: 7170 us -> 8180 us (1.14)
  waiting for transfers between devices: 2890 us -> 3990 us
  blocking collectives: 3630 us -> 3500 us
    psum x0 -> x1, waiting for transfers between devices: none -> 1060 us  [shards(): lax.psum(lax.psum((shares[0], shares[1], shares[2], shares[3], shares[4],...]
    psum x1, blocking collectives: 975 us -> 848 us  [shards(): lax.psum((shares[0], shares[1], shares[2], shares[3], shares[4], shares[5...]
    unnamed x12 -> x13, waiting for transfers between devices: 1110 us -> 1110 us
  transfers between devices with their start and end apart: 10 -> 11, of which waited for: 8 -> 9; matrix products, arithmetic and copies ran while one was open for 7% -> 6% of each run, Pallas kernels for 0% -> 0%
where the time goes in v1:
time: 8180 us; the launch traced here: 8170 us
  waiting for transfers between devices  3990 us (49%)
  blocking collectives  3500 us (43%)
  matrix products  356 us (4%)
  local copies, waits for them, and re-layouts  197 us (2%)
  other arithmetic  84.4 us (1%)
    psum x1, blocking collectives, shards(): lax.psum((key_grad_all[:, :SUMM], value_grad_all[:, :SUMM]), 'ctx')  2490 us
    unnamed x13, waiting for transfers between devices  1110 us
    psum x1, waiting for transfers between devices, shards(): lax.psum(lax.psum((shares[0], shares[1], shares[2], shares[3], shares[4],...  1060 us
    psum x1, blocking collectives, shards(): lax.psum((shares[0], shares[1], shares[2], shares[3], shares[4], shares[5...  848 us
    all_gather x1, waiting for transfers between devices, shards(): lax.all_gather(up_weight, 'fsdp', axis=0, tiled=True)  553 us
    all_gather x1, waiting for transfers between devices, shards(): lax.all_gather(down_weight, 'fsdp', axis=0, tiled=True)  526 us
    all_gather x1, waiting for transfers between devices, shards(): lax.all_gather(qkv_weight, 'fsdp', axis=0, tiled=True)  337 us
    reduce_scatter x1, waiting for transfers between devices, shards(): lax.psum_scatter(qkv_weight_grad.astype(jnp.bfloat16), 'fsdp', scatter_di...  310 us
  transfers between devices with their start and end apart: 11, of which 9 were waited for; matrix products, arithmetic and copies ran while one was open for 6% of the time, Pallas kernels for 0%

profile of v1, /device:TPU:1, one launch (start us, length us, event | category | flops | bytes accessed | tf_op | source)
XLA Modules:
  0.0 8166.6 jit_solution(13841071836612689876)
XLA Ops:
  8.7 10.3 all-gather.3
  29.7 36.0 all-gather.5
  66.3 33.2 all-gather.4
  100.8 336.6 %all-gather.17.cloned.1.call-done = bf16[2048,6144]{1,0:T(8,128)(2,1)} async-done(((bf16[512,6144]{1,0:T(8,128)(2,1)}), bf16[2048,6144]{1,0:T(8,128)(2,1)}) %all-gather.17.cloned.1.call-update) | async-done | bytes 25165840 | tf_op jit(solution)/shard_map/all_gather | solution.py:79
  437.4 11.9 fusion.87
  469.3 10.2 all_gather.61
  540.9 48.1 while.26
  588.9 88.7 %all-gather.19.cloned.1.call-done = bf16[2048,2048]{1,0:T(8,128)(2,1)} async-done(((bf16[512,2048]{1,0:T(8,128)(2,1)}), bf16[2048,2048]{1,0:T(8,128)(2,1)}) %all-gather.19.cloned.1.call-update) | async-done | bytes 8388624 | tf_op jit(solution)/shard_map/all_gather | solution.py:82
  686.1 552.7 %all-gather.21.cloned.1.call-done = bf16[2048,8192]{1,0:T(8,128)(2,1)} async-done(((bf16[512,8192]{1,0:T(8,128)(2,1)}), bf16[2048,8192]{1,0:T(8,128)(2,1)}) %all-gather.21.cloned.1.call-update) | async-done | bytes 33554448 | tf_op jit(solution)/shard_map/all_gather | solution.py:86
  1238.8 34.7 multiply_convert_fusion.1
  1273.4 526.4 %all-gather.23.cloned.1.call-done = bf16[8192,2048]{1,0:T(8,128)(2,1)} async-done(((bf16[2048,2048]{1,0:T(8,128)(2,1)}), bf16[8192,2048]{1,0:T(8,128)(2,1)}) %all-gather.23.cloned.1.call-update) | async-done | bytes 33554448 | tf_op jit(solution)/shard_map/all_gather | solution.py:88
  1799.8 36.4 fusion.83
  1836.2 17.0 multiply_reduce_fusion.1
  1870.1 188.6 %while.27 = (s32[]{:T(128)}, bf16[4,1,272,512]{2,3,1,0:T(8,128)(2,1)}, f32[4,1,1138,512]{2,3,1,0:T(8,128)}, f32[4,1,1138,512]{2,3,1,0:T(8,128)}, s32[4]{0:T(128)...) while((s32[]{:T(128)}, ...), condition=%wide.region_14.15_spmd, body=%wide.region_12.14_spmd.sunk | while | flops 1604632448 | bytes 115616344 | solution.py:240
  2077.6 21.4 copy.74
  2099.0 21.4 copy.73
  2120.5 2492.1 %all-reduce.25 = (bf16[1,50,2048]{2,0,1:T(2,128)(2,1)S(1)}, bf16[1,50,2048]{2,0,1:T(2,128)(2,1)S(1)}, bf16[1,1088,2048]{2,0,1:T(2,128)(2,1)}, bf16[1,1088,2048]{2,0,1:T(2,128)(2,1)}) all-reduce(f32[1,50,2048]{2,0,1:T(1,128)S(1)} %copy.76, f32[1,50,2048]{2,0,1:T(1,128)S(1)} %copy.75, ...), channel_id=1, replica_groups=mesh['fsdp'=4,'replica'=2,'ctx'=4] {'ctx'}, use_global_device_ids=true, to_apply=%region_20.21 | all-reduce | flops 4661248 | bytes 27967488 | tf_op jit(solution)/shard_map/psum | solution.py:248
  4629.2 17.1 convolution_convert_fusion.2
  4648.0 24.3 convolution_convert_fusion.1
  4673.5 24.3 convolution_convert_fusion
  4704.3 12.2 fusion.69
  4716.6 14.9 fusion.40
  4731.5 17.9 all-reduce.19
  4750.0 310.0 %reduce-scatter.9.cloned.1.call-done = bf16[512,6144]{1,0:T(8,128)(2,1)} async-done(((bf16[2048,6144]{1,0:T(8,128)(2,1)}), bf16[512,6144]{1,0:T(8,128)(2,1)}) %reduce-scatter.9.cloned.1.call-update) | async-done | bytes 6291472 | tf_op jit(solution)/shard_map/reduce_scatter | solution.py:298
  5060.1 556.3 %reduce-scatter.13.cloned.1.call-done = bf16[512,8192]{1,0:T(8,128)(2,1)} async-done(((bf16[2048,8192]{1,0:T(8,128)(2,1)}), bf16[512,8192]{1,0:T(8,128)(2,1)}) %reduce-scatter.13.cloned.1.call-update) | async-done | bytes 8388624
  5616.3 555.0 %reduce-scatter.15.cloned.1.call-done = bf16[2048,2048]{1,0:T(8,128)(2,1)} async-done(((bf16[8192,2048]{1,0:T(8,128)(2,1)}), bf16[2048,2048]{1,0:T(8,128)(2,1)}) %reduce-scatter.15.cloned.1.call-update) | async-done | bytes 8388624
  6171.4 848.1 %all-reduce.26 = (f32[512]{0:T(512)S(1)}, f32[512]{0:T(512)S(1)}, f32[512,6144]{1,0:T(8,128)}, f32[512]{0:T(512)S(1)}, f32[512]{0:T(512)S(1)}, /*index=5*/f32[51...) all-reduce(f32[512]{0:T(512)S(1)} %dynamic-slice_convert_fusion.8, ...), channel_id=1, replica_groups=mesh['fsdp'=4,'replica'=2,'ctx'=4] {'ctx'}, use_global_device_ids=true, to_apply=%region_26.27 | all-reduce | flops 12589056 | bytes 75546624 | tf_op jit(solution)/shard_map/psum | solution.py:327
  7020.1 10.2 all-gather.9
  7037.4 17.2 fusion.31
  7063.0 1061.6 %all-reduce.24.cloned.1.call-done = (f32[512,6144]{1,0:T(8,128)}, f32[512,2048]{1,0:T(8,128)}, f32[512,8192]{1,0:T(8,128)}, f32[2048,2048]{1,0:T(8,128)}) async-done(((f32[512,6144]{1,0:T(8,128)}, f32[512,2048]{1,0:T(8,128)}, f32[512,8192]{1,0:T(8,128)}, f32[2048,2048]{1,0:T(8,128)}), (f32[512,6144]{1,0:T(8,128)}, f32[512,2048]{1,0:T(8,128)}, f32[512,8192]{1,0:T(8,128)}, ...) | async-done | bytes 50331664 | tf_op jit(solution)/shard_map/psum | solution.py:326
  8124.6 11.0 copy.140
  8137.7 13.9 copy.142
  (372 shorter events, 412.2 us)
Async XLA Ops:
  7.2 92.4 %copy-start.2 = (bf16[1,272,2048]{2,1,0:T(8,128)(2,1)S(1)}, bf16[1,272,2048]{2,1,0:T(8,128)(2,1)}, u32[]{:S(2)}) copy-start(bf16[1,272,2048]{2,1,0:T(8,128)(2,1)} %param.21) | copy-start | bytes 3342340
  7.2 430.2 %all-gather.17.cloned.1.call-start = ((), (), s32[]{:S(2)}) async-start(), calls=%async_computation.4 | async-start | bytes 31457280 | tf_op jit(solution)/shard_map/all_gather | solution.py:79
  7.9 502.7 %all-gather.25.cloned.1.call-start = ((), (), s32[]{:S(2)}) async-start(), calls=%async_computation.10 | async-start | bytes 5570560 | tf_op jit(solution)/shard_map/all_gather | solution.py:131
  29.0 472.0 %copy-start.26 = (f32[4,1,512]{2,1,0:T(1,128)}, f32[4,1,512]{2,1,0:T(1,128)S(1)}, u32[]{:S(2)}) copy-start(f32[4,1,512]{2,1,0:T(1,128)S(1)} %convert_element_type.263) | copy-start | bytes 24580
  99.8 349.5 %copy-start.30 = (f32[272]{0:T(512)}, f32[272]{0:T(512)S(1)}, u32[]{:S(2)}) copy-start(f32[272]{0:T(512)S(1)} %broadcast_multiply_fusion.5) | copy-start | bytes 3268
  100.3 349.0 %copy-start.34 = (f32[272]{0:T(512)}, f32[272]{0:T(512)S(1)}, u32[]{:S(2)}) copy-start(f32[272]{0:T(512)S(1)} %add_rsqrt_fusion.1) | copy-start | bytes 3268
  100.8 348.5 %copy-start.19 = (bf16[272,2048]{1,0:T(8,128)(2,1)}, bf16[272,2048]{1,0:T(8,128)(2,1)S(1)}, u32[]{:S(2)}) copy-start(bf16[272,2048]{1,0:T(8,128)(2,1)S(1)} %fusion.34) | copy-start | bytes 3342340
  454.1 72.7 all-gather.27.cloned.1.call-start
  457.0 220.7 %all-gather.19.cloned.1.call-start = ((), (), s32[]{:S(2)}) async-start(), calls=%async_computation.5 | async-start | bytes 10485760 | tf_op jit(solution)/shard_map/all_gather | solution.py:82
  457.6 21.9 copy-start.50
  457.6 31.6 copy-start.51
  457.6 41.0 copy-start.54
  457.6 42.2 copy-start.18
  457.6 781.1 %all-gather.21.cloned.1.call-start = ((), (), s32[]{:S(2)}) async-start(), calls=%async_computation.6 | async-start | bytes 41943040 | tf_op jit(solution)/shard_map/all_gather | solution.py:86
  458.2 1341.6 %all-gather.23.cloned.1.call-start = ((), (), s32[]{:S(2)}) async-start(), calls=%async_computation.7 | async-start | bytes 41943040 | tf_op jit(solution)/shard_map/all_gather | solution.py:88
  458.8 4291.2 %reduce-scatter.11.cloned.1.call-start = ((), (), s32[]{:S(2)}) async-start(), calls=%async_computation.9 | async-start | bytes 10485760 | tf_op jit(solution)/shard_map/reduce_scatter | solution.py:307
  489.2 749.5 %copy-start.40 = (f32[4,1,512]{2,1,0:T(1,128)}, f32[4,1,512]{2,1,0:T(1,128)S(1)}, u32[]{:S(2)}) copy-start(f32[4,1,512]{2,1,0:T(1,128)S(1)} %convert_element_type.269) | copy-start | bytes 24580
  498.5 1354.8 %copy-start.28 = (f32[4,1,512]{2,1,0:T(1,128)}, f32[4,1,512]{2,1,0:T(1,128)S(1)}, u32[]{:S(2)}) copy-start(f32[4,1,512]{2,1,0:T(1,128)S(1)} %convert_element_type.268) | copy-start | bytes 24580
  588.9 95.4 %copy-start = (pred[1,1,272,1138]{3,2,1,0:T(8,128)(4,1)}, pred[1,1,272,1138]{3,2,1,0:T(8,128)(4,1)S(1)}, u32[]{:S(2)}) copy-start(pred[1,1,272,1138]{3,2,1,0:T(8,128)(4,1)S(1)} %get-tuple-element.590) | copy-start | bytes 928612
  588.9 95.4 %copy-start.7 = (bf16[1,272,2048]{1,2,0:T(8,128)(2,1)}, bf16[1,272,2048]{1,2,0:T(8,128)(2,1)S(1)}, u32[]{:S(2)}) copy-start(bf16[1,272,2048]{1,2,0:T(8,128)(2,1)S(1)} %get-tuple-element.599) | copy-start | bytes 3342340
  684.3 1169.0 %copy-start.32 = (f32[272]{0:T(512)}, f32[272]{0:T(512)S(1)}, u32[]{:S(2)}) copy-start(f32[272]{0:T(512)S(1)} %broadcast_multiply_fusion.4) | copy-start | bytes 3268
  686.1 1167.2 %copy-start.38 = (f32[272]{0:T(512)}, f32[272]{0:T(512)S(1)}, u32[]{:S(2)}) copy-start(f32[272]{0:T(512)S(1)} %add_rsqrt_fusion) | copy-start | bytes 3268
  1238.8 561.0 %copy-start.13 = (bf16[1,272,2048]{2,1,0:T(8,128)(2,1)S(1)}, bf16[1,272,2048]{2,1,0:T(8,128)(2,1)}, u32[]{:S(2)}) copy-start(bf16[1,272,2048]{2,1,0:T(8,128)(2,1)} %param.24) | copy-start | bytes 3342340
  1799.8 36.4 copy-start.5
  1836.2 17.1 copy-start.14
  1861.6 3198.4 %reduce-scatter.9.cloned.1.call-start = ((), (), s32[]{:S(2)}) async-start(), calls=%async_computation.8 | async-start | bytes 31457280 | tf_op jit(solution)/shard_map/reduce_scatter | solution.py:298
  4646.4 970.0 %reduce-scatter.13.cloned.1.call-start = ((), (), s32[]{:S(2)}) async-start(), calls=%async_computation.12 | async-start | bytes 41943040
  4672.3 1499.1 %reduce-scatter.15.cloned.1.call-start = ((), (), s32[]{:S(2)}) async-start(), calls=%async_computation.13 | async-start | bytes 41943040
  4697.8 3426.8 %all-reduce.24.cloned.1.call-start = ((), (), s32[]{:S(2)}) async-start(), calls=%async_computation.14 | async-start | bytes 100663296 | tf_op jit(solution)/shard_map/psum | solution.py:326
  7020.1 17.3 slice-start.9
  8135.6 16.0 slice-start.2
  8137.7 16.0 slice-start.5
  (51 other events, 338.5 us)
Sparse Core Ops, SparseCore 0:
  9.6 427.7 all-gather.16
  454.2 34.3 all-gather.24
  490.8 35.9 all-gather.26
  528.2 149.4 all-gather.18
  679.1 559.6 all-gather.20
  1240.2 559.5 all-gather.22
  1861.7 142.2 reduce-scatter.10
  4646.5 413.5 reduce-scatter.8
  5062.5 553.7 reduce-scatter.12
  5618.5 552.7 reduce-scatter.14
  7019.6 1104.9 all-reduce.23
